TPU v7x, 256 devices: a whole 4x4x8 slice. The times are simulated.
256 devices in a mesh: xg: 4 (over x_hi, core), yd: 64 (over x_lo, z, y).
Axes of the slice: x: 4 (x_hi: 2, x_lo: 2; x = x_hi * 2 + x_lo), y: 4, z: 8, core: 2. Of those that a mesh axis runs over, the one named last changes fastest.
Arguments:
- mobile: float32 [4096, 1, 1024], P('yd', None, 'xg'), may hold values from 0 to 2
- dispersion_x: float32 [4096, 1, 1024], P('yd', None, 'xg'), may hold values from 0.5 to 200000
- dispersion_y: float32 [4096, 1, 1024], P('yd', None, 'xg'), may hold values from 0.5 to 200000
- capacity: float32 [4096, 1, 1024], P('yd', None, 'xg'), may hold values from 0.5 to 8
- immobile: float32 [4, 4096, 1, 1024], P(None, 'yd', None, 'xg'), may hold values from 0 to 2
- exchange_rates: float32 [4], replicated, may hold values from 0.02 to 50
- rate_shares: float32 [4], replicated, may hold values from 0.1 to 1
Outputs:
- updated: float32 [4096, 1, 1024], P('yd', None, 'xg')
All inputs are finite; a program needn't handle non-finite values.
Results may differ from a plain program's by a relative error of at most 0.0003.
Values sent between devices are 32-bit elements; how exact they have to be, the bound alone decides.
A program may use at most 64 MiB of HBM per device.

v0:
```python
import jax
import jax.numpy as jnp
from jax import lax
from jax.sharding import PartitionSpec as P


def shifted_2(value, axis, steps):
    count = lax.axis_size(axis)
    pairs = [(source, (source + steps) % count) for source in range(count)]
    return lax.ppermute(value, axis, pairs)


def shifted(values, stride, axis, filling):
    length = values.shape[axis]
    if stride > 0:
        kept_part = lax.slice_in_dim(values, 0, length - stride, axis=axis)
        filler = jnp.full_like(lax.slice_in_dim(values, 0, stride, axis=axis), filling)
        return jnp.concatenate([filler, kept_part], axis=axis)
    backward = -stride
    kept_part = lax.slice_in_dim(values, backward, length, axis=axis)
    filler = jnp.full_like(lax.slice_in_dim(values, 0, backward, axis=axis), filling)
    return jnp.concatenate([kept_part, filler], axis=axis)


def pick_at(values, position, axis):
    return lax.index_in_dim(values, position, axis, keepdims=False)


def periodic_solve(face_coef, storage, right_side, axis):
    length = right_side.shape[axis]
    sub_coef = -face_coef
    super_coef = -jnp.roll(face_coef, -1, axis)
    main_coef = storage + face_coef - super_coef
    stride = 1
    while stride < length // 2:
        sub_left = jnp.roll(sub_coef, stride, axis)
        main_left = jnp.roll(main_coef, stride, axis)
        super_left = jnp.roll(super_coef, stride, axis)
        side_left = jnp.roll(right_side, stride, axis)
        sub_right = jnp.roll(sub_coef, -stride, axis)
        main_right = jnp.roll(main_coef, -stride, axis)
        super_right = jnp.roll(super_coef, -stride, axis)
        side_right = jnp.roll(right_side, -stride, axis)
        left_ratio = sub_coef / main_left
        right_ratio = super_coef / main_right
        main_coef = main_coef - left_ratio * super_left - right_ratio * sub_right
        right_side = right_side - left_ratio * side_left - right_ratio * side_right
        sub_coef = -left_ratio * sub_left
        super_coef = -right_ratio * super_right
        stride = stride * 2
    coupling = sub_coef + super_coef
    main_other = jnp.roll(main_coef, stride, axis)
    coupling_other = jnp.roll(coupling, stride, axis)
    side_other = jnp.roll(right_side, stride, axis)
    return (right_side * main_other - coupling * side_other) / (
        main_coef * main_other - coupling * coupling_other
    )


def block_solve(face_coef, storage, source, axis):
    length = source.shape[axis]
    position = lax.broadcasted_iota(jnp.int32, source.shape, axis)
    at_first = position == 0
    at_last = position == length - 1
    following = shifted(face_coef, -1, axis, 0.0)
    nothing = jnp.zeros_like(source)
    sub_coef = jnp.where(at_first | at_last, nothing, -face_coef)
    super_coef = jnp.where(at_last, nothing, -following)
    main_coef = jnp.where(at_last, 1.0, storage + face_coef + following)
    right_side = jnp.stack(
        [
            jnp.where(at_last, nothing, source),
            jnp.where(at_first, face_coef, nothing),
            jnp.where(at_last, 1.0, nothing),
        ]
    )
    stride = 1
    while stride < length:
        sub_left = shifted(sub_coef, stride, axis, 0.0)
        main_left = shifted(main_coef, stride, axis, 1.0)
        super_left = shifted(super_coef, stride, axis, 0.0)
        side_left = shifted(right_side, stride, axis + 1, 0.0)
        sub_right = shifted(sub_coef, -stride, axis, 0.0)
        main_right = shifted(main_coef, -stride, axis, 1.0)
        super_right = shifted(super_coef, -stride, axis, 0.0)
        side_right = shifted(right_side, -stride, axis + 1, 0.0)
        left_ratio = sub_coef / main_left
        right_ratio = super_coef / main_right
        right_side = right_side - left_ratio[None] * side_left - right_ratio[None] * side_right
        main_coef = main_coef - left_ratio * super_left - right_ratio * sub_right
        sub_coef = -left_ratio * sub_left
        super_coef = -right_ratio * super_right
        stride = stride * 2
    return right_side / main_coef[None]


def reduced_rows(solved, face_coef, storage, source, upcoming, axis):
    from_next, face_next = upcoming
    length = source.shape[axis]
    face_last = pick_at(face_coef, length - 1, axis)
    sub_last = -face_last
    super_last = -face_next
    main_last = pick_at(storage, length - 1, axis) + face_last + face_next
    coef_prev = sub_last * pick_at(solved[1], length - 2, axis)
    coef_self = (
        main_last + sub_last * pick_at(solved[2], length - 2, axis) + super_last * from_next[1]
    )
    coef_next = super_last * from_next[2]
    target = (
        pick_at(source, length - 1, axis)
        - sub_last * pick_at(solved[0], length - 2, axis)
        - super_last * from_next[0]
    )
    return (coef_prev, coef_self, coef_next, target)


def dense_cyclic(all_rows, group_size):
    matrix_rows = []
    targets = []
    for row_index in range(group_size):
        entries = [jnp.zeros_like(all_rows[row_index, 1]) for column in range(group_size)]
        entries[(row_index - 1) % group_size] = all_rows[row_index, 0]
        entries[row_index] = all_rows[row_index, 1]
        entries[(row_index + 1) % group_size] = all_rows[row_index, 2]
        matrix_rows.append(entries)
        targets.append(all_rows[row_index, 3])
    for pivot in range(group_size):
        for row_index in range(pivot + 1, group_size):
            factor = matrix_rows[row_index][pivot] / matrix_rows[pivot][pivot]
            matrix_rows[row_index] = [
                matrix_rows[row_index][column] - factor * matrix_rows[pivot][column]
                for column in range(group_size)
            ]
            targets[row_index] = targets[row_index] - factor * targets[pivot]
    solutions = [None] * group_size
    for row_index in reversed(range(group_size)):
        total = targets[row_index]
        for column in range(row_index + 1, group_size):
            total = total - matrix_rows[row_index][column] * solutions[column]
        solutions[row_index] = total / matrix_rows[row_index][row_index]
    return jnp.stack(solutions)


def local(mobile, dispersion_x, dispersion_y, capacity, immobile, exchange_rates, rate_shares):
    weights = rate_shares * exchange_rates / (1.0 + exchange_rates)
    gain_terms = capacity[None] * weights[:, None, None, None]
    storage = 1.0 + jnp.sum(gain_terms, axis=0)
    source = mobile + jnp.sum(gain_terms * immobile, axis=0)
    solved = block_solve(dispersion_x, storage, source, 2)
    head_values = pick_at(solved, 0, 3)
    upcoming = shifted_2((head_values, pick_at(dispersion_x, 0, 2)), "xg", -1)
    rows = reduced_rows(solved, dispersion_x, storage, source, upcoming, 2)
    group_size = lax.axis_size("xg")
    all_rows = lax.all_gather(jnp.stack(rows)[None], "xg", axis=0, tiled=True)
    solutions = dense_cyclic(all_rows, group_size)
    own_index = lax.axis_index("xg")
    own_value = lax.dynamic_index_in_dim(solutions, own_index, 0, keepdims=False)
    prev_value = lax.dynamic_index_in_dim(
        solutions, (own_index + group_size - 1) % group_size, 0, keepdims=False
    )
    after_x = solved[0] + solved[1] * prev_value[..., None] + solved[2] * own_value[..., None]
    group_count = lax.axis_size("yd")

    def regroup(values):
        return values.reshape(values.shape[0], group_count, -1)

    line_values = lax.all_to_all(regroup(after_x), "yd", split_axis=1, concat_axis=0, tiled=True)
    line_faces = lax.all_to_all(
        regroup(dispersion_y), "yd", split_axis=1, concat_axis=0, tiled=True
    )
    line_storage = lax.all_to_all(regroup(storage), "yd", split_axis=1, concat_axis=0, tiled=True)
    solved_lines = periodic_solve(line_faces, line_storage, line_storage * line_values, 0)
    updated = lax.all_to_all(solved_lines, "yd", split_axis=0, concat_axis=1, tiled=True)
    updated = updated.reshape(after_x.shape)
    return updated


def solution(mesh):
    return jax.shard_map(
        local,
        mesh=mesh,
        in_specs=(
            P("yd", None, "xg"),
            P("yd", None, "xg"),
            P("yd", None, "xg"),
            P("yd", None, "xg"),
            P(None, "yd", None, "xg"),
            P(),
            P(),
        ),
        out_specs=P("yd", None, "xg"),
        check_vma=False,
    )
```

profile of v0, /device:TPU:4, one launch (start us, length us, event | category | flops | bytes accessed | tf_op | source)
XLA Modules:
  0.0 107.0 jit_solution(12925277914980473333)
XLA Ops:
  0.0 0.8 copy.95
  0.9 0.8 copy.55
  2.5 1.6 %fusion = (f32[64,256]{1,0:T(8,128)S(1)}, f32[64,256]{1,0:T(8,128)S(1)}) fusion(f32[4,64,1,256]{3,2,1,0:T(1,128)} %param.11, f32[64,256]{1,0:T(8,128)S(1)} %bitcast.400, f32[4]{0:T(128)S(1)} %add_divide_fusion), kind=kLoop, calls=%fused_computation.2 | loop fusion | flops 229376 | bytes 458768 | tf_op jit(solution)/shard_map/reduce_sum | solution.py:148
  4.1 0.9 add_select_fusion
  5.1 0.9 fusion.90
  12.3 2.4 %collective-permute-start = (f32[64,1]{0,1:T(1,128)S(1)}, f32[64,1]{0,1:T(1,128)S(1)}, u32[]{:S(2)}, u32[]{:S(2)}) collective-permute-start(f32[64,1]{0,1:T(1,128)S(1)} %bitcast.403), channel_id=1, source_target_pairs={{0,192},{64,0},{128,64},{192,128},{1,193},{65,1},{129,65},{193,129... | collective-permute-start | bytes 776 | tf_op jit(solution)/shard_map/ppermute | solution.py:10
  14.8 0.8 reshape.21111
  15.6 11.9 %all-to-all-start.2 = ((f32[64,1,256]{2,1,0:T(1,128)}), f32[64,1,256]{2,1,0:T(1,128)S(1)}, u32[]{:S(2)}, u32[]{:S(2)}) async-start(f32[64,1,256]{2,1,0:T(1,128)} %reshape.21111), calls=%async_computation.2 | async-start | bytes 131072 | tf_op jit(solution)/shard_map/all_to_all | solution.py:168
  28.2 0.8 reshape.21113
  29.0 6.7 %all-gather = f32[16,64,1]{1,2,0:T(1,128)S(1)} all-gather(f32[4,64,1]{1,2,0:T(1,128)S(1)} %pad_maximum_fusion.2), channel_id=2, replica_groups=mesh['xg'=4,'yd'=64] {'xg'}, dimensions={0}, use_global_device_ids=true | all-gather | bytes 5120 | tf_op jit(solution)/shard_map/all_gather | solution.py:154
  35.9 0.8 reshape.21115
  36.6 1.7 %all-to-all-done.2 = f32[64,1,256]{2,1,0:T(1,128)S(1)} async-done(((f32[64,1,256]{2,1,0:T(1,128)}), f32[64,1,256]{2,1,0:T(1,128)S(1)}, u32[]{:S(2)}, u32[]{:S(2)}) %all-to-all-start.2) | async-done | bytes 65568 | tf_op jit(solution)/shard_map/all_to_all | solution.py:168
  38.3 9.6 %all-to-all-start = ((f32[64,1,256]{2,1,0:T(1,128)}), f32[64,1,256]{2,1,0:T(1,128)S(1)}, u32[]{:S(2)}, u32[]{:S(2)}) async-start(f32[64,1,256]{2,1,0:T(1,128)} %reshape.21113), calls=%async_computation | async-start | bytes 131072 | tf_op jit(solution)/shard_map/all_to_all | solution.py:171
  48.5 0.8 reduce.15
  49.6 9.1 %all-to-all-done = f32[64,1,256]{2,1,0:T(1,128)S(1)} async-done(((f32[64,1,256]{2,1,0:T(1,128)}), f32[64,1,256]{2,1,0:T(1,128)S(1)}, u32[]{:S(2)}, u32[]{:S(2)}) %all-to-all-start) | async-done | bytes 65568 | tf_op jit(solution)/shard_map/all_to_all | solution.py:171
  58.7 4.8 %all-to-all-start.1 = ((f32[64,1,256]{2,1,0:T(1,128)}), f32[64,1,256]{2,1,0:T(1,128)S(1)}, u32[]{:S(2)}, u32[]{:S(2)}) async-start(f32[64,1,256]{2,1,0:T(1,128)} %reshape.21115), calls=%async_computation.1 | async-start | bytes 131072 | tf_op jit(solution)/shard_map/all_to_all | solution.py:167
  63.5 0.8 reduce.14
  64.5 9.5 %all-to-all-done.1 = f32[64,1,256]{2,1,0:T(1,128)S(1)} async-done(((f32[64,1,256]{2,1,0:T(1,128)}), f32[64,1,256]{2,1,0:T(1,128)S(1)}, u32[]{:S(2)}, u32[]{:S(2)}) %all-to-all-start.1) | async-done | bytes 65568 | tf_op jit(solution)/shard_map/all_to_all | solution.py:167
  74.1 0.8 reduce.16
  85.0 1.7 %reshape.21117 = f32[64,1,256]{2,1,0:T(1,128)S(1)} reshape(f32[4096,4]{1,0:T(8,128)S(1)} %copy.96) | data formatting | bytes 131072
  86.7 14.6 %all_to_all.69 = f32[64,1,256]{2,1,0:T(1,128)S(1)} all-to-all(f32[64,1,256]{2,1,0:T(1,128)S(1)} %reshape.21117), channel_id=1, replica_groups=mesh['xg'=4,'yd'=64] {'yd'}, dimensions={0} | all-to-all | bytes 131072 | tf_op jit(solution)/shard_map/all_to_all | solution.py:173
  101.3 0.8 reduce.18
  102.1 3.4 %reshape.21118 = f32[4096,1,4]{2,1,0:T(1,128)S(1)} reshape(f32[64,256]{1,0:T(8,128)S(1)} %reduce.18) | data formatting | bytes 131072
  106.3 0.7 copy.85
  (228 shorter events, 19.2 us)
Async XLA Ops:
  0.0 6.0 %copy-start = (f32[64,1,256]{2,1,0:T(1,128)S(1)}, f32[64,1,256]{2,1,0:T(1,128)}, u32[]{:S(2)}) copy-start(f32[64,1,256]{2,1,0:T(1,128)} %param.8) | copy-start | bytes 196612
  11.1 3.6 %copy-start.1 = (f32[64,1,256]{2,1,0:T(1,128)S(1)}, f32[64,1,256]{2,1,0:T(1,128)}, u32[]{:S(2)}) copy-start(f32[64,1,256]{2,1,0:T(1,128)} %param.9) | copy-start | bytes 196612
  11.7 17.3 %collective-permute-start.1 = (f32[3,64,1]{1,2,0:T(1,128)S(1)}, f32[3,64,1]{1,2,0:T(1,128)S(1)}, u32[]{:S(2)}, u32[]{:S(2)}) collective-permute-start(f32[3,64,1]{1,2,0:T(1,128)S(1)} %squeeze.95), channel_id=1, source_target_pairs={{0,192},{64,0},{128,64},{192,128},{1,193},{65,1},{129,65},{193,129... | collective-permute-start | bytes 2312 | tf_op jit(solution)/shard_map/ppermute | solution.py:10
  12.3 16.7 %collective-permute-start = (f32[64,1]{0,1:T(1,128)S(1)}, f32[64,1]{0,1:T(1,128)S(1)}, u32[]{:S(2)}, u32[]{:S(2)}) collective-permute-start(f32[64,1]{0,1:T(1,128)S(1)} %bitcast.403), channel_id=1, source_target_pairs={{0,192},{64,0},{128,64},{192,128},{1,193},{65,1},{129,65},{193,129... | collective-permute-start | bytes 776 | tf_op jit(solution)/shard_map/ppermute | solution.py:10
  15.6 22.7 %all-to-all-start.2 = ((f32[64,1,256]{2,1,0:T(1,128)}), f32[64,1,256]{2,1,0:T(1,128)S(1)}, u32[]{:S(2)}, u32[]{:S(2)}) async-start(f32[64,1,256]{2,1,0:T(1,128)} %reshape.21111), calls=%async_computation.2 | async-start | bytes 131072 | tf_op jit(solution)/shard_map/all_to_all | solution.py:168
  38.3 20.4 %all-to-all-start = ((f32[64,1,256]{2,1,0:T(1,128)}), f32[64,1,256]{2,1,0:T(1,128)S(1)}, u32[]{:S(2)}, u32[]{:S(2)}) async-start(f32[64,1,256]{2,1,0:T(1,128)} %reshape.21113), calls=%async_computation | async-start | bytes 131072 | tf_op jit(solution)/shard_map/all_to_all | solution.py:171
  58.7 15.4 %all-to-all-start.1 = ((f32[64,1,256]{2,1,0:T(1,128)}), f32[64,1,256]{2,1,0:T(1,128)S(1)}, u32[]{:S(2)}, u32[]{:S(2)}) async-start(f32[64,1,256]{2,1,0:T(1,128)} %reshape.21115), calls=%async_computation.1 | async-start | bytes 131072 | tf_op jit(solution)/shard_map/all_to_all | solution.py:167
where the time goes:
time: 108 us; the launch traced here: 107 us
  starting transfers between devices  28.8 us (27%)
  local copies, waits for them, and re-layouts  21.3 us (20%)
  blocking collectives  21.3 us (20%)
  waiting for transfers between devices  20.3 us (19%)
  other arithmetic  14.1 us (13%)
  between operations  1.29 us (1%)
    all_to_all x1, blocking collectives, local(): lax.all_to_all(solved_lines, 'yd', split_axis=0, concat_axis=1, tiled=True)  14.6 us
    all_to_all x1, starting transfers between devices, local(): lax.all_to_all(regroup(dispersion_y), 'yd', split_axis=1, concat_axis=0,...  11.9 us
    unnamed x16, local copies, waits for them, and re-layouts  10.2 us
    all_to_all x1, starting transfers between devices, local(): lax.all_to_all(regroup(storage), 'yd', split_axis=1, concat_axis=0, tiled...  9.63 us
    all_to_all x1, waiting for transfers between devices, local(): lax.all_to_all(regroup(after_x), 'yd', split_axis=1, concat_axis=0, tiled...  9.53 us
    all_to_all x1, waiting for transfers between devices, local(): lax.all_to_all(regroup(storage), 'yd', split_axis=1, concat_axis=0, tiled...  9.06 us
    all_gather x1, blocking collectives, local(): all_rows = lax.all_gather(jnp.stack(rows)[None], 'xg', axis=0, tiled=True)  6.7 us
    all_to_all x1, starting transfers between devices, local(): lax.all_to_all(regroup(after_x), 'yd', split_axis=1, concat_axis=0, tiled...  4.8 us
  transfers between devices with their start and end apart: 5, of which 3 were waited for; matrix products, arithmetic and copies ran while one was open for 6% of the time, Pallas kernels for 0%

commit v1 on v0

--- a/solution.py
+++ b/solution.py
@@ -151,7 +151,9 @@
     upcoming = shifted_2((head_values, pick_at(dispersion_x, 0, 2)), "xg", -1)
     rows = reduced_rows(solved, dispersion_x, storage, source, upcoming, 2)
     group_size = lax.axis_size("xg")
-    all_rows = lax.all_gather(jnp.stack(rows)[None], "xg", axis=0, tiled=True)
+    all_rows = jnp.concatenate(
+        lax.all_to_all(jnp.stack([jnp.stack(rows)[None]] * lax.axis_size("xg")), "xg", 0, 0), axis=0
+    )
     solutions = dense_cyclic(all_rows, group_size)
     own_index = lax.axis_index("xg")
     own_value = lax.dynamic_index_in_dim(solutions, own_index, 0, keepdims=False)

time: 108 us -> 114 us (1.056); the launches traced: 107 us -> 112 us
  waiting for transfers between devices: 20.3 us -> 28.6 us
  blocking collectives: 21.3 us -> 14.6 us
  starting transfers between devices: 28.8 us -> 30.3 us
    all_to_all x1, waiting for transfers between devices: 1.66 us -> 8.5 us  [local(): lax.all_to_all(regroup(dispersion_y), 'yd', split_axis=1, concat_axis=0,...]
    all_gather x1 -> x0, blocking collectives: 6.7 us -> none  [local(): all_rows = lax.all_gather(jnp.stack(rows)[None], 'xg', axis=0, tiled=True)]
    all_to_all x0 -> x1, starting transfers between devices: none -> 5.8 us  [local(): lax.all_to_all(jnp.stack([jnp.stack(rows)[None]] * lax.axis_size('xg')),...]
    all_to_all x1, starting transfers between devices: 9.63 us -> 4.62 us  [local(): lax.all_to_all(regroup(storage), 'yd', split_axis=1, concat_axis=0, tiled...]
    unnamed x16 -> x19, local copies, waits for them, and re-layouts: 10.2 us -> 10.9 us
  transfers between devices with their start and end apart: 5 -> 6, of which waited for: 3 -> 4; matrix products, arithmetic and copies ran while one was open for 6% -> 6% of each run, Pallas kernels for 0% -> 0%
where the time goes in v1:
time: 114 us; the launch traced here: 112 us
  starting transfers between devices  30.3 us (27%)
  waiting for transfers between devices  28.6 us (25%)
  local copies, waits for them, and re-layouts  22.1 us (19%)
  other arithmetic  15.1 us (13%)
  blocking collectives  14.6 us (13%)
  between operations  1.27 us (1%)
    all_to_all x1, blocking collectives, local(): lax.all_to_all(solved_lines, 'yd', split_axis=0, concat_axis=1, tiled=True)  14.6 us
    all_to_all x1, starting transfers between devices, local(): lax.all_to_all(regroup(dispersion_y), 'yd', split_axis=1, concat_axis=0,...  12.7 us
    unnamed x19, local copies, waits for them, and re-layouts  10.9 us
    all_to_all x1, waiting for transfers between devices, local(): lax.all_to_all(regroup(storage), 'yd', split_axis=1, concat_axis=0, tiled...  9.57 us
    all_to_all x1, waiting for transfers between devices, local(): lax.all_to_all(regroup(after_x), 'yd', split_axis=1, concat_axis=0, tiled...  9.5 us
    all_to_all x1, waiting for transfers between devices, local(): lax.all_to_all(regroup(dispersion_y), 'yd', split_axis=1, concat_axis=0,...  8.5 us
    all_to_all x1, starting transfers between devices, local(): lax.all_to_all(jnp.stack([jnp.stack(rows)[None]] * lax.axis_size('xg')),...  5.8 us
    all_to_all x1, starting transfers between devices, local(): lax.all_to_all(regroup(after_x), 'yd', split_axis=1, concat_axis=0, tiled...  4.73 us
  transfers between devices with their start and end apart: 6, of which 4 were waited for; matrix products, arithmetic and copies ran while one was open for 6% of the time, Pallas kernels for 0%

profile of v1, /device:TPU:4, one launch (start us, length us, event | category | flops | bytes accessed | tf_op | source)
XLA Modules:
  0.0 111.9 jit_solution(11693296545759484907)
XLA Ops:
  0.0 0.8 copy.47
  0.9 0.8 copy.23
  2.5 1.6 %fusion = (f32[64,256]{1,0:T(8,128)S(1)}, f32[64,256]{1,0:T(8,128)S(1)}) fusion(f32[4,64,1,256]{3,2,1,0:T(1,128)} %param.11, f32[64,256]{1,0:T(8,128)S(1)} %bitcast.404, f32[4]{0:T(128)S(1)} %add_divide_fusion), kind=kLoop, calls=%fused_computation.2 | loop fusion | flops 229376 | bytes 458768 | tf_op jit(solution)/shard_map/reduce_sum | solution.py:148
  4.1 0.9 add_select_fusion
  5.1 0.9 fusion.90
  12.3 2.4 %collective-permute-start = (f32[64,1]{0,1:T(1,128)S(1)}, f32[64,1]{0,1:T(1,128)S(1)}, u32[]{:S(2)}, u32[]{:S(2)}) collective-permute-start(f32[64,1]{0,1:T(1,128)S(1)} %bitcast.407), channel_id=1, source_target_pairs={{0,192},{64,0},{128,64},{192,128},{1,193},{65,1},{129,65},{193,129... | collective-permute-start | bytes 776 | tf_op jit(solution)/shard_map/ppermute | solution.py:10
  15.0 1.0 collective-permute-done
  16.7 5.8 %all-to-all-start.1 = ((f32[4,1,256]{2,1,0:T(1,128)}), f32[4,1,256]{2,1,0:T(1,128)S(1)}, u32[]{:S(2)}, u32[]{:S(2)}) async-start(f32[4,1,256]{2,1,0:T(1,128)} %reshape.21121), calls=%async_computation.1 | async-start | bytes 8192 | tf_op jit(solution)/shard_map/all_to_all | solution.py:155
  22.9 0.8 reshape.21119
  23.8 0.8 reshape.21117
  24.6 12.7 %all-to-all-start.3 = ((f32[64,1,256]{2,1,0:T(1,128)}), f32[64,1,256]{2,1,0:T(1,128)S(1)}, u32[]{:S(2)}, u32[]{:S(2)}) async-start(f32[64,1,256]{2,1,0:T(1,128)} %reshape.21117), calls=%async_computation.3 | async-start | bytes 131072 | tf_op jit(solution)/shard_map/all_to_all | solution.py:170
  38.8 0.8 reshape.21123
  39.6 8.5 %all-to-all-done.3 = f32[64,1,256]{2,1,0:T(1,128)S(1)} async-done(((f32[64,1,256]{2,1,0:T(1,128)}), f32[64,1,256]{2,1,0:T(1,128)S(1)}, u32[]{:S(2)}, u32[]{:S(2)}) %all-to-all-start.3) | async-done | bytes 65568 | tf_op jit(solution)/shard_map/all_to_all | solution.py:170
  48.1 4.6 %all-to-all-start = ((f32[64,1,256]{2,1,0:T(1,128)}), f32[64,1,256]{2,1,0:T(1,128)S(1)}, u32[]{:S(2)}, u32[]{:S(2)}) async-start(f32[64,1,256]{2,1,0:T(1,128)} %reshape.21119), calls=%async_computation | async-start | bytes 131072 | tf_op jit(solution)/shard_map/all_to_all | solution.py:173
  52.7 0.8 reduce.15
  53.9 9.6 %all-to-all-done = f32[64,1,256]{2,1,0:T(1,128)S(1)} async-done(((f32[64,1,256]{2,1,0:T(1,128)}), f32[64,1,256]{2,1,0:T(1,128)S(1)}, u32[]{:S(2)}, u32[]{:S(2)}) %all-to-all-start) | async-done | bytes 65568 | tf_op jit(solution)/shard_map/all_to_all | solution.py:173
  63.5 4.7 %all-to-all-start.2 = ((f32[64,1,256]{2,1,0:T(1,128)}), f32[64,1,256]{2,1,0:T(1,128)S(1)}, u32[]{:S(2)}, u32[]{:S(2)}) async-start(f32[64,1,256]{2,1,0:T(1,128)} %reshape.21123), calls=%async_computation.2 | async-start | bytes 131072 | tf_op jit(solution)/shard_map/all_to_all | solution.py:169
  68.2 0.8 reduce.14
  69.3 9.5 %all-to-all-done.2 = f32[64,1,256]{2,1,0:T(1,128)S(1)} async-done(((f32[64,1,256]{2,1,0:T(1,128)}), f32[64,1,256]{2,1,0:T(1,128)S(1)}, u32[]{:S(2)}, u32[]{:S(2)}) %all-to-all-start.2) | async-done | bytes 65568 | tf_op jit(solution)/shard_map/all_to_all | solution.py:169
  78.8 0.8 reduce.17
  89.8 1.7 %reshape.21125 = f32[64,1,256]{2,1,0:T(1,128)S(1)} reshape(f32[4096,4]{1,0:T(8,128)S(1)} %copy.48) | data formatting | bytes 131072
  91.6 14.6 %all_to_all.74 = f32[64,1,256]{2,1,0:T(1,128)S(1)} all-to-all(f32[64,1,256]{2,1,0:T(1,128)S(1)} %reshape.21125), channel_id=1, replica_groups=mesh['xg'=4,'yd'=64] {'yd'}, dimensions={0} | all-to-all | bytes 131072 | tf_op jit(solution)/shard_map/all_to_all | solution.py:175
  106.1 0.8 reduce.19
  107.0 3.4 %reshape.21126 = f32[4096,1,4]{2,1,0:T(1,128)S(1)} reshape(f32[64,256]{1,0:T(8,128)S(1)} %reduce.19) | data formatting | bytes 131072
  (234 shorter events, 21.5 us)
Async XLA Ops:
  0.0 6.0 %copy-start = (f32[64,1,256]{2,1,0:T(1,128)S(1)}, f32[64,1,256]{2,1,0:T(1,128)}, u32[]{:S(2)}) copy-start(f32[64,1,256]{2,1,0:T(1,128)} %param.8) | copy-start | bytes 196612
  11.5 12.2 %copy-start.1 = (f32[64,1,256]{2,1,0:T(1,128)S(1)}, f32[64,1,256]{2,1,0:T(1,128)}, u32[]{:S(2)}) copy-start(f32[64,1,256]{2,1,0:T(1,128)} %param.9) | copy-start | bytes 196612
  11.7 4.3 %collective-permute-start.1 = (f32[3,64,1]{1,2,0:T(1,128)S(1)}, f32[3,64,1]{1,2,0:T(1,128)S(1)}, u32[]{:S(2)}, u32[]{:S(2)}) collective-permute-start(f32[3,64,1]{1,2,0:T(1,128)S(1)} %squeeze.95), channel_id=1, source_target_pairs={{0,192},{64,0},{128,64},{192,128},{1,193},{65,1},{129,65},{193,129... | collective-permute-start | bytes 2312 | tf_op jit(solution)/shard_map/ppermute | solution.py:10
  12.3 3.7 %collective-permute-start = (f32[64,1]{0,1:T(1,128)S(1)}, f32[64,1]{0,1:T(1,128)S(1)}, u32[]{:S(2)}, u32[]{:S(2)}) collective-permute-start(f32[64,1]{0,1:T(1,128)S(1)} %bitcast.407), channel_id=1, source_target_pairs={{0,192},{64,0},{128,64},{192,128},{1,193},{65,1},{129,65},{193,129... | collective-permute-start | bytes 776 | tf_op jit(solution)/shard_map/ppermute | solution.py:10
  16.7 7.9 %all-to-all-start.1 = ((f32[4,1,256]{2,1,0:T(1,128)}), f32[4,1,256]{2,1,0:T(1,128)S(1)}, u32[]{:S(2)}, u32[]{:S(2)}) async-start(f32[4,1,256]{2,1,0:T(1,128)} %reshape.21121), calls=%async_computation.1 | async-start | bytes 8192 | tf_op jit(solution)/shard_map/all_to_all | solution.py:155
  24.6 23.5 %all-to-all-start.3 = ((f32[64,1,256]{2,1,0:T(1,128)}), f32[64,1,256]{2,1,0:T(1,128)S(1)}, u32[]{:S(2)}, u32[]{:S(2)}) async-start(f32[64,1,256]{2,1,0:T(1,128)} %reshape.21117), calls=%async_computation.3 | async-start | bytes 131072 | tf_op jit(solution)/shard_map/all_to_all | solution.py:170
  48.1 15.4 %all-to-all-start = ((f32[64,1,256]{2,1,0:T(1,128)}), f32[64,1,256]{2,1,0:T(1,128)S(1)}, u32[]{:S(2)}, u32[]{:S(2)}) async-start(f32[64,1,256]{2,1,0:T(1,128)} %reshape.21119), calls=%async_computation | async-start | bytes 131072 | tf_op jit(solution)/shard_map/all_to_all | solution.py:173
  63.5 15.3 %all-to-all-start.2 = ((f32[64,1,256]{2,1,0:T(1,128)}), f32[64,1,256]{2,1,0:T(1,128)S(1)}, u32[]{:S(2)}, u32[]{:S(2)}) async-start(f32[64,1,256]{2,1,0:T(1,128)} %reshape.21123), calls=%async_computation.2 | async-start | bytes 131072 | tf_op jit(solution)/shard_map/all_to_all | solution.py:169
